TPU v7x, 32 devices: a whole 2x2x4 slice. The times are simulated.
32 devices in a mesh: inst: 4 (over y, x), row: 2 (over core), pitch: 4 (over z).
Axes of the slice: x: 2, y: 2, z: 4, core: 2. Of those that a mesh axis runs over, the one named last changes fastest.
Arguments:
- direction: float32 [4, 5, 12288], P('inst', None, ('row', 'pitch')), may hold values from -6 to 6
- time_matrix: float32 [4, 4], replicated, may hold values from -3 to 3
- volume: float32 [12288], P(('row', 'pitch')), may hold values from 0.5 to 2
- diag_jac: float32 [4, 25, 12288], P('inst', None, ('row', 'pitch')), may hold values from -2.5 to 2.5
- face_jac: float32 [4, 50, 24576], P('inst', None, ('row', 'pitch')), may hold values from -1 to 1
- face_left: int32 [24576], P(('row', 'pitch')), may hold values from 0 to 1535
- face_right: int32 [24576], P(('row', 'pitch')), may hold values from 0 to 1535
- bound_jac: float32 [4, 4, 50, 3072], P('inst', None, None, ('row', 'pitch')), may hold values from -1 to 1
- bound_cell: int32 [4, 3072], P(None, ('row', 'pitch')), may hold values from 0 to 1535
- send_cell: int32 [4, 3072], P(None, ('row', 'pitch')), may hold values from 0 to 1535
Outputs:
- product: float32 [4, 5, 12288], P('inst', None, ('row', 'pitch'))
Inputs may be any that keep to these rules, and one draw needn't show every extreme that they name: `face_left`: a cell index local to the face's block of 1536 cells. `face_right`: a cell index local to the face's block of 1536 cells. `bound_cell`: a cell index local to the face's block of 1536 cells. `send_cell`: a cell index local to the supplying block of 1536 cells.
All inputs are finite; a program needn't handle non-finite values.
Results may differ from a plain program's by a relative error of at most 0.000052.
Values sent between devices are 32-bit elements; how exact they have to be, the bound alone decides.
A program may use at most 128 MiB of HBM per device.

v0:
```python
import functools
import jax
import jax.numpy as jnp
from jax import lax
from jax.experimental import pallas as pl
from jax.experimental.pallas import tpu as pltpu
from jax.sharding import PartitionSpec as P

LANE = 128
COMP = 5
TERMS = 2 * COMP
PACK = 16
GROUP = 4
MESH = pl.DeviceIdType.MESH


def gathered(own, cell):
    low = cell & (LANE - 1)
    high = cell >> 7
    chunks = own.shape[1] * GROUP
    masks = [high == h for h in range(chunks)]
    values = []
    for b in range(COMP):
        found = None
        for h in range(chunks):
            row = own[b, h // GROUP, pl.ds(h % GROUP, 1), :]
            part = jnp.take_along_axis(
                jnp.broadcast_to(row, cell.shape), low, axis=1, mode="promise_in_bounds"
            )
            found = part if h == 0 else jnp.where(masks[h], part, found)
        values.append(found)
    return values


def applied(block, base, values):
    result = []
    for a in range(COMP):
        total = None
        for b in range(COMP):
            term = block(base + COMP * a + b) * values[b]
            total = term if total is None else total + term
        result.append(total)
    return result


def two_terms(value):
    first = value.astype(jnp.bfloat16).astype(jnp.float32)
    return first, value - first


def packed_row(row):
    return jnp.broadcast_to(row, (PACK, LANE)).astype(jnp.bfloat16)


def hot_tile(hot, place, cell_row, value):
    low = packed_row((cell_row & (LANE - 1)).astype(jnp.float32))
    for s in range(0, LANE, PACK):
        index = lax.broadcasted_iota(jnp.int32, (PACK, LANE), 0) + s
        index = index.astype(jnp.float32).astype(jnp.bfloat16)
        hot[s : s + PACK, place : place + LANE] = jnp.where(
            index == low, jnp.bfloat16(value), jnp.bfloat16(0)
        )


def chunk_mask(cell_row):
    index = lax.broadcasted_iota(jnp.int32, (PACK, LANE), 0)
    index = index.astype(jnp.float32).astype(jnp.bfloat16)
    return index == packed_row((cell_row >> 7).astype(jnp.float32))


def kernel(
    n_inst,
    n_row,
    n_pitch,
    tm_hbm,
    dir_hbm,
    vol_hbm,
    diag_hbm,
    face_hbm,
    left_hbm,
    right_hbm,
    bound_hbm,
    bcell_hbm,
    scell_hbm,
    out_ref,
    tm_ref,
    own,
    vol_line,
    vol,
    diag,
    face,
    left,
    right,
    bound,
    bcell,
    scell,
    dirs,
    ghost_out,
    ghost_in,
    flux_terms,
    bound_terms,
    rows,
    hot,
    acc,
    local_sem,
    inst_send,
    inst_recv,
    ghost_send,
    ghost_recv,
):
    t = lax.axis_index("inst")
    r = lax.axis_index("row")
    p = lax.axis_index("pitch")
    blocks = own.shape[1]
    chunks = blocks * GROUP
    f_tiles = left.shape[0]
    faces = f_tiles * LANE
    bounds = bcell.shape[1]
    b_tiles = bounds // LANE

    barrier = pltpu.get_barrier_semaphore()

    def greet(**place):
        pl.semaphore_signal(barrier, inc=1, device_id=place, device_id_type=MESH)

    up = lax.rem(p + 1, n_pitch)
    down = lax.rem(p + n_pitch - 1, n_pitch)
    greet(pitch=up)
    greet(pitch=down)

    @pl.when(r > 0)
    def _():
        greet(row=r - 1)

    @pl.when(r < n_row - 1)
    def _():
        greet(row=r + 1)

    for o in range(1, n_inst):
        greet(inst=lax.rem(t + o, n_inst))

    pairs = [
        (dir_hbm, own),
        (scell_hbm, scell),
        (bcell_hbm, bcell),
        (left_hbm, left),
        (right_hbm, right),
        (face_hbm, face),
        (bound_hbm, bound),
        (diag_hbm, diag),
        (vol_hbm, vol_line),
        (tm_hbm, tm_ref),
    ]
    copies = [
        pltpu.make_async_copy(a, b, local_sem.at[i]) for i, (a, b) in enumerate(pairs)
    ]
    for c in copies:
        c.start()

    for c in copies[0:3]:
        c.wait()
    inner = []
    for j in range(b_tiles):
        at = slice(j * LANE, (j + 1) * LANE)
        values = gathered(own, jnp.concatenate([scell[:, at], bcell[:, at]], axis=0))
        for b in range(COMP):
            ghost_out[j, pl.ds(b, GROUP, stride=8), :] = values[b][0:GROUP]
        inner.append([v[GROUP : 2 * GROUP] for v in values])

    greeted = 2 + n_inst - 1
    extra = jnp.where(r > 0, 1, 0) + jnp.where(r < n_row - 1, 1, 0)
    pl.semaphore_wait(barrier, greeted + extra)

    def ghost_copy(k, **place):
        opposite = k ^ 1
        return pltpu.make_async_remote_copy(
            src_ref=ghost_out.at[:, 8 * k : 8 * k + COMP],
            dst_ref=ghost_in.at[:, 8 * opposite : 8 * opposite + COMP],
            send_sem=ghost_send.at[k],
            recv_sem=ghost_recv.at[opposite],
            device_id=place,
            device_id_type=MESH,
        )

    to_down = ghost_copy(0, pitch=down)
    to_up = ghost_copy(1, pitch=up)
    to_down.start()
    to_up.start()

    @pl.when(r > 0)
    def _():
        ghost_copy(2, row=r - 1).start()

    @pl.when(r < n_row - 1)
    def _():
        ghost_copy(3, row=r + 1).start()

    sends = []
    for o in range(1, n_inst):
        c = pltpu.make_async_remote_copy(
            src_ref=own,
            dst_ref=dirs.at[o],
            send_sem=inst_send.at[o],
            recv_sem=inst_recv.at[o],
            device_id={"inst": lax.rem(t + o, n_inst)},
            device_id_type=MESH,
        )
        c.start()
        sends.append(c)

    @pl.when(r == 0)
    def _():
        ghost_in[:, 16:24, :] = jnp.zeros((b_tiles, 8, LANE), jnp.float32)

    @pl.when(r == n_row - 1)
    def _():
        ghost_in[:, 24:32, :] = jnp.zeros((b_tiles, 8, LANE), jnp.float32)

    for c in copies[3:10]:
        c.wait()

    def product(start, size):
        return lax.dot_general(
            rows[:, start : start + size],
            hot[:, start : start + size],
            (((1,), (1,)), ((), ())),
            preferred_element_type=jnp.float32,
        )

    total = None
    for g in range(0, f_tiles, 8):
        block = lambda i, g=g: face[i, g : g + 8, :]
        cell_l = left[g : g + 8, :]
        cell_r = right[g : g + 8, :]
        one = applied(block, 0, gathered(own, cell_l))
        two = applied(block, COMP * COMP, gathered(own, cell_r))
        for a in range(COMP):
            first, rest = two_terms(one[a] + two[a])
            flux_terms[a, g : g + 8, :] = first
            flux_terms[COMP + a, g : g + 8, :] = rest
        for s in range(g, g + 8):
            place = 2 * s * LANE
            row_l = left[s : s + 1, :]
            row_r = right[s : s + 1, :]
            hot_tile(hot, place, row_l, 1.0)
            hot_tile(hot, place + LANE, row_r, -1.0)
            mask_l = chunk_mask(row_l)
            mask_r = chunk_mask(row_r)
            for a in range(TERMS):
                value = packed_row(flux_terms[a, s : s + 1, :])
                at = slice(a * PACK, (a + 1) * PACK)
                zero = jnp.bfloat16(0)
                rows[at, place : place + LANE] = jnp.where(mask_l, value, zero)
                rows[at, place + LANE : place + 2 * LANE] = jnp.where(mask_r, value, zero)
        part = product(2 * g * LANE, 16 * LANE)
        total = part if total is None else total + part
    acc[...] = total

    def boundary_place(j, k):
        pair = 1 - k // 2
        return 2 * faces + 2 * pair * bounds + (2 * j + k % 2) * LANE

    inner_flux = []
    for j in range(b_tiles):
        at = slice(j * LANE, (j + 1) * LANE)
        inner_flux.append(applied(lambda i, at=at: bound[i, :, at], 0, inner[j]))
        for k in range(GROUP):
            hot_tile(hot, boundary_place(j, k), bcell[k : k + 1, at], 1.0)
    for h in range(chunks):
        vol[h // GROUP, pl.ds(h % GROUP, 1), :] = vol_line[
            h * LANE : (h + 1) * LANE
        ].reshape(1, LANE)

    for q in range(blocks):
        local = applied(lambda i, q=q: diag[i, q], 0, [own[b, q] for b in range(COMP)])
        for a in range(COMP):
            out_ref[a, q] = local[a] + (tm_ref[t, t] * own[a, q]) * vol[q]

    def boundary(start):
        for j in range(b_tiles):
            at = slice(j * LANE, (j + 1) * LANE)
            outer = [
                ghost_in[j, pl.ds(8 * start + b, 2, stride=8), :] for b in range(COMP)
            ]
            block = lambda i, at=at: bound[i, start : start + 2, at]
            flux = applied(block, COMP * COMP, outer)
            for a in range(COMP):
                first, rest = two_terms(inner_flux[j][a][start : start + 2] + flux[a])
                bound_terms[a, j, start : start + 2, :] = first
                bound_terms[COMP + a, j, start : start + 2, :] = rest
            for k in range(start, start + 2):
                place = boundary_place(j, k)
                mask = chunk_mask(bcell[k : k + 1, at])
                for a in range(TERMS):
                    value = packed_row(bound_terms[a, j, pl.ds(k, 1), :])
                    rows[a * PACK : (a + 1) * PACK, place : place + LANE] = jnp.where(
                        mask, value, jnp.bfloat16(0)
                    )

    @pl.when(r > 0)
    def _():
        ghost_copy(2, row=r - 1).wait_send()
        half = ghost_in.at[:, 16 : 16 + COMP]
        pltpu.make_async_copy(half, half, ghost_recv.at[2]).wait()

    @pl.when(r < n_row - 1)
    def _():
        ghost_copy(3, row=r + 1).wait_send()
        half = ghost_in.at[:, 24 : 24 + COMP]
        pltpu.make_async_copy(half, half, ghost_recv.at[3]).wait()

    boundary(2)
    acc[...] = acc[...] + product(2 * faces, 2 * bounds)

    for c in sends:
        c.wait()
    weights = [tm_ref[t, lax.rem(t + n_inst - o, n_inst)] for o in range(1, n_inst)]
    for q in range(blocks):
        for a in range(COMP):
            mixed = None
            for o in range(1, n_inst):
                term = weights[o - 1] * dirs[o, a, q]
                mixed = term if mixed is None else mixed + term
            at = a * PACK + q * GROUP
            both = acc[at : at + GROUP, :]
            at = at + COMP * PACK
            both = both + acc[at : at + GROUP, :]
            out_ref[a, q] = out_ref[a, q] + mixed * vol[q] + both

    to_down.wait()
    to_up.wait()
    boundary(0)
    acc[...] = product(2 * faces + 2 * bounds, 2 * bounds)
    for q in range(blocks):
        for a in range(COMP):
            at = a * PACK + q * GROUP
            both = acc[at : at + GROUP, :]
            at = at + COMP * PACK
            out_ref[a, q] = out_ref[a, q] + (both + acc[at : at + GROUP, :])


def per_device(
    direction,
    time_matrix,
    volume,
    diag_jac,
    face_jac,
    face_left,
    face_right,
    bound_jac,
    bound_cell,
    send_cell,
):
    n_inst = lax.axis_size("inst")
    n_row = lax.axis_size("row")
    n_pitch = lax.axis_size("pitch")
    cells = direction.shape[2]
    faces = face_left.shape[0]
    bounds = bound_cell.shape[1]
    blocks = cells // (GROUP * LANE)
    f_tiles = faces // LANE
    b_tiles = bounds // LANE
    width = 2 * faces + 4 * bounds
    f32, i32, bf16 = jnp.float32, jnp.int32, jnp.bfloat16
    cell_view = (blocks, GROUP, LANE)
    hbm = pl.BlockSpec(memory_space=pl.ANY)
    result = pl.pallas_call(
        functools.partial(kernel, n_inst, n_row, n_pitch),
        out_shape=pltpu.VMEM((COMP, *cell_view), f32),
        in_specs=[hbm] * 10,
        out_specs=pl.BlockSpec(memory_space=pltpu.VMEM),
        scratch_shapes=[
            pltpu.SMEM((n_inst, n_inst), f32),
            pltpu.VMEM((COMP, *cell_view), f32),
            pltpu.VMEM((cells,), f32),
            pltpu.VMEM(cell_view, f32),
            pltpu.VMEM((25, *cell_view), f32),
            pltpu.VMEM((50, f_tiles, LANE), f32),
            pltpu.VMEM((f_tiles, LANE), i32),
            pltpu.VMEM((f_tiles, LANE), i32),
            pltpu.VMEM((50, 4, bounds), f32),
            pltpu.VMEM((4, bounds), i32),
            pltpu.VMEM((4, bounds), i32),
            pltpu.VMEM((n_inst, COMP, *cell_view), f32),
            pltpu.VMEM((b_tiles, 32, LANE), f32),
            pltpu.VMEM((b_tiles, 32, LANE), f32),
            pltpu.VMEM((TERMS, f_tiles, LANE), f32),
            pltpu.VMEM((TERMS, b_tiles, GROUP, LANE), f32),
            pltpu.VMEM((TERMS * PACK, width), bf16),
            pltpu.VMEM((LANE, width), bf16),
            pltpu.VMEM((TERMS * PACK, LANE), f32),
            pltpu.SemaphoreType.DMA((10,)),
            pltpu.SemaphoreType.DMA((n_inst,)),
            pltpu.SemaphoreType.DMA((n_inst,)),
            pltpu.SemaphoreType.DMA((4,)),
            pltpu.SemaphoreType.DMA((4,)),
        ],
        compiler_params=pltpu.CompilerParams(collective_id=0, has_side_effects=True),
    )(
        time_matrix,
        direction[0].reshape(COMP, *cell_view),
        volume,
        diag_jac[0].reshape(25, *cell_view),
        face_jac[0].reshape(50, f_tiles, LANE),
        face_left.reshape(f_tiles, LANE),
        face_right.reshape(f_tiles, LANE),
        bound_jac[0].transpose(1, 0, 2),
        bound_cell,
        send_cell,
    )
    return result.reshape(1, COMP, cells)


def solution(mesh):
    return jax.shard_map(
        per_device,
        mesh=mesh,
        in_specs=(
            P("inst", None, ("row", "pitch")),
            P(),
            P(("row", "pitch")),
            P("inst", None, ("row", "pitch")),
            P("inst", None, ("row", "pitch")),
            P(("row", "pitch")),
            P(("row", "pitch")),
            P("inst", None, None, ("row", "pitch")),
            P(None, ("row", "pitch")),
            P(None, ("row", "pitch")),
        ),
        out_specs=P("inst", None, ("row", "pitch")),
        check_vma=False,
    )
```

profile of v0, /device:TPU:0, one launch (start us, length us, event | category | flops | bytes accessed | tf_op | source)
XLA Modules:
  0.0 10.6 jit_solution(12329330197145887847)
XLA Ops:
  0.0 10.0 %shard_map.100 = f32[5,3,4,128]{3,2,1,0:T(4,128)S(1)} custom-call(f32[4,4]{1,0:T(4,128)} %tm_hbm.1, f32[5,3,4,128]{3,2,1,0:T(4,128)} %bitcast.13, f32[1536]{0:T(1024)} %vol_hbm.1, f32[25,3,4,128]{3,2,1,0:T(4,128)} %bitcast.12, f32[50,24,128]{2,1,0:T(8,128)} %bitcast.10, s32[24,128]{1,0:T(8,128)} %bitcast.14, s32[24,128]{1,0:T(8,128)} %bitcast.15, ...), custom_call_target="tpu_custom_call" | custom-call | tf_op jit(solution)/shard_map/pallas_call | solution.py:367
  10.0 0.6 %copy.14 = f32[1,5,1536]{2,0,1:T(1,128)} copy(f32[1,5,1536]{2,0,1:T(1,128)S(1)} %bitcast.9) | data formatting | bytes 61440
where the time goes:
time: 10.7 us; the launch traced here: 10.6 us
  Pallas kernels  9.97 us (93%)
  local copies, waits for them, and re-layouts  0.61 us (6%)
    pallas_call x1, Pallas kernels, per_device(): pl.pallas_call(functools.partial(kernel, n_inst, n_row, n_pitch), out_sha...  9.97 us
    unnamed x1, local copies, waits for them, and re-layouts  0.61 us

commit v1 on v0

--- a/solution.py
+++ b/solution.py
@@ -68,7 +68,18 @@
     return index == packed_row((cell_row >> 7).astype(jnp.float32))
 
 
-def kernel(
+NEAR, LATE, BELOW, ABOVE = 0, 1, 2, 3
+
+
+def kernel(n_inst, n_row, n_pitch, *refs):
+    pl.run_scoped(
+        functools.partial(body, n_inst, n_row, n_pitch, *refs),
+        pltpu.SemaphoreType.DMA((10,)),
+        pltpu.SemaphoreType.DMA((n_inst + 8,)),
+    )
+
+
+def body(
     n_inst,
     n_row,
     n_pitch,
@@ -93,20 +104,22 @@
     right,
     bound,
     bcell,
-    scell,
     dirs,
-    ghost_out,
-    ghost_in,
+    ghost,
+    ghost_cell,
+    late_jac,
+    inner_flux,
+    place_cell,
     flux_terms,
     bound_terms,
     rows,
     hot,
     acc,
+    inst_recv,
+    ghost_recv,
+    ready,
     local_sem,
-    inst_send,
-    inst_recv,
-    ghost_send,
-    ghost_recv,
+    send_sem,
 ):
     t = lax.axis_index("inst")
     r = lax.axis_index("row")
@@ -115,33 +128,44 @@
     chunks = blocks * GROUP
     f_tiles = left.shape[0]
     faces = f_tiles * LANE
-    bounds = bcell.shape[1]
-    b_tiles = bounds // LANE
+    b_tiles = bcell.shape[0]
+    bounds = b_tiles * LANE
+    last = n_inst - 1
 
     barrier = pltpu.get_barrier_semaphore()
 
-    def greet(**place):
-        pl.semaphore_signal(barrier, inc=1, device_id=place, device_id_type=MESH)
+    def signal(sem, **place):
+        pl.semaphore_signal(sem, inc=1, device_id=place, device_id_type=MESH)
 
     up = lax.rem(p + 1, n_pitch)
     down = lax.rem(p + n_pitch - 1, n_pitch)
-    greet(pitch=up)
-    greet(pitch=down)
-
-    @pl.when(r > 0)
-    def _():
-        greet(row=r - 1)
+
+    down_first = jnp.logical_and(p >= 1, p <= n_pitch - 2)
+    up_first = p >= n_pitch - 2
+
+    @pl.when(jnp.logical_not(down_first))
+    def _():
+        signal(barrier, pitch=down)
+
+    @pl.when(jnp.logical_not(up_first))
+    def _():
+        signal(barrier, pitch=up)
 
     @pl.when(r < n_row - 1)
     def _():
-        greet(row=r + 1)
-
-    for o in range(1, n_inst):
-        greet(inst=lax.rem(t + o, n_inst))
+        signal(barrier, row=r + 1)
+
+    @pl.when(t == 0)
+    def _():
+        for u in range(1, n_inst):
+            signal(barrier, inst=u)
+
+    @pl.when(jnp.logical_and(t > 0, t < last))
+    def _():
+        signal(barrier, inst=last)
 
     pairs = [
         (dir_hbm, own),
-        (scell_hbm, scell),
         (bcell_hbm, bcell),
         (left_hbm, left),
         (right_hbm, right),
@@ -154,69 +178,94 @@
     copies = [
         pltpu.make_async_copy(a, b, local_sem.at[i]) for i, (a, b) in enumerate(pairs)
     ]
-    for c in copies:
-        c.start()
-
-    for c in copies[0:3]:
-        c.wait()
-    inner = []
-    for j in range(b_tiles):
-        at = slice(j * LANE, (j + 1) * LANE)
-        values = gathered(own, jnp.concatenate([scell[:, at], bcell[:, at]], axis=0))
-        for b in range(COMP):
-            ghost_out[j, pl.ds(b, GROUP, stride=8), :] = values[b][0:GROUP]
-        inner.append([v[GROUP : 2 * GROUP] for v in values])
-
-    greeted = 2 + n_inst - 1
-    extra = jnp.where(r > 0, 1, 0) + jnp.where(r < n_row - 1, 1, 0)
-    pl.semaphore_wait(barrier, greeted + extra)
-
-    def ghost_copy(k, **place):
-        opposite = k ^ 1
+
+    def ghost_copies(slot, at, **place):
+        return [
+            pltpu.make_async_remote_copy(
+                src_ref=a,
+                dst_ref=b,
+                send_sem=send_sem.at[at + i],
+                recv_sem=ghost_recv.at[slot],
+                device_id=place,
+                device_id_type=MESH,
+            )
+            for i, (a, b) in enumerate(
+                [(dir_hbm, ghost.at[slot, 0:COMP]), (scell_hbm, ghost_cell.at[slot])]
+            )
+        ]
+
+    def to_up():
+        return ghost_copies(jnp.where(p == n_pitch - 1, LATE, NEAR), n_inst, pitch=up)
+
+    def to_down():
+        return ghost_copies(jnp.where(p == 1, NEAR, LATE), n_inst + 2, pitch=down)
+
+    def to_below():
+        return ghost_copies(ABOVE, n_inst + 4, row=r - 1)
+
+    def to_above():
+        return ghost_copies(BELOW, n_inst + 6, row=r + 1)
+
+    def start(group):
+        for c in group:
+            c.start()
+
+    def inst_copy(o):
         return pltpu.make_async_remote_copy(
-            src_ref=ghost_out.at[:, 8 * k : 8 * k + COMP],
-            dst_ref=ghost_in.at[:, 8 * opposite : 8 * opposite + COMP],
-            send_sem=ghost_send.at[k],
-            recv_sem=ghost_recv.at[opposite],
-            device_id=place,
-            device_id_type=MESH,
-        )
-
-    to_down = ghost_copy(0, pitch=down)
-    to_up = ghost_copy(1, pitch=up)
-    to_down.start()
-    to_up.start()
-
-    @pl.when(r > 0)
-    def _():
-        ghost_copy(2, row=r - 1).start()
-
-    @pl.when(r < n_row - 1)
-    def _():
-        ghost_copy(3, row=r + 1).start()
-
-    sends = []
-    for o in range(1, n_inst):
-        c = pltpu.make_async_remote_copy(
-            src_ref=own,
+            src_ref=dir_hbm,
             dst_ref=dirs.at[o],
-            send_sem=inst_send.at[o],
-            recv_sem=inst_recv.at[o],
+            send_sem=send_sem.at[o],
+            recv_sem=inst_recv.at[0],
             device_id={"inst": lax.rem(t + o, n_inst)},
             device_id_type=MESH,
         )
-        c.start()
-        sends.append(c)
+
+    def inst_first(o):
+        return jnp.logical_or(lax.rem(t + o, n_inst) == 0, t == last)
+
+    greeted = jnp.where(t == last, last, jnp.where(t > 0, 1, 0))
+    greeted = greeted + jnp.where(r > 0, 1, 0)
+    greeted = greeted + jnp.where(down_first, 1, 0) + jnp.where(up_first, 1, 0)
+
+    @pl.when(greeted > 0)
+    def _():
+        pl.semaphore_wait(barrier, greeted)
+
+    @pl.when(up_first)
+    def _():
+        start(to_up())
+        signal(ready.at[2], pitch=up)
+
+    for o in range(1, n_inst):
+
+        @pl.when(inst_first(o))
+        def _(o=o):
+            inst_copy(o).start()
+            signal(ready.at[0], inst=lax.rem(t + o, n_inst))
+
+    @pl.when(down_first)
+    def _():
+        start(to_down())
+        signal(ready.at[1], pitch=down)
+
+    @pl.when(r > 0)
+    def _():
+        start(to_below())
+        signal(ready.at[0], row=r - 1)
+
+    start(copies)
 
     @pl.when(r == 0)
     def _():
-        ghost_in[:, 16:24, :] = jnp.zeros((b_tiles, 8, LANE), jnp.float32)
+        ghost[BELOW] = jnp.zeros(ghost.shape[1:], jnp.float32)
+        ghost_cell[BELOW] = jnp.zeros(ghost_cell.shape[1:], jnp.int32)
 
     @pl.when(r == n_row - 1)
     def _():
-        ghost_in[:, 24:32, :] = jnp.zeros((b_tiles, 8, LANE), jnp.float32)
-
-    for c in copies[3:10]:
+        ghost[ABOVE] = jnp.zeros(ghost.shape[1:], jnp.float32)
+        ghost_cell[ABOVE] = jnp.zeros(ghost_cell.shape[1:], jnp.int32)
+
+    for c in copies:
         c.wait()
 
     def product(start, size):
@@ -256,16 +305,30 @@
         total = part if total is None else total + part
     acc[...] = total
 
-    def boundary_place(j, k):
-        pair = 1 - k // 2
-        return 2 * faces + 2 * pair * bounds + (2 * j + k % 2) * LANE
-
-    inner_flux = []
+    edge = p == 0
+
+    def side(slot, pick):
+        if slot >= BELOW:
+            return pick(slot)
+        if slot == NEAR:
+            return jnp.where(edge, pick(1), pick(0))
+        return jnp.where(edge, pick(0), pick(1))
+
+    def boundary_place(slot, j):
+        return 2 * faces + ((3 - slot) * b_tiles + j) * LANE
+
     for j in range(b_tiles):
-        at = slice(j * LANE, (j + 1) * LANE)
-        inner_flux.append(applied(lambda i, at=at: bound[i, :, at], 0, inner[j]))
-        for k in range(GROUP):
-            hot_tile(hot, boundary_place(j, k), bcell[k : k + 1, at], 1.0)
+        block = lambda i, j=j: bound[i, j]
+        flux = applied(block, 0, gathered(own, bcell[j]))
+        for a in range(COMP):
+            inner_flux[a, j] = flux[a]
+    for slot in range(4):
+        place_cell[slot] = side(slot, lambda k: bcell[:, k, :])
+        for j in range(b_tiles):
+            hot_tile(hot, boundary_place(slot, j), place_cell[slot, j : j + 1, :], 1.0)
+    for i in range(COMP * COMP):
+        late_jac[i] = side(LATE, lambda k, i=i: bound[COMP * COMP + i, :, k, :])
+
     for h in range(chunks):
         vol[h // GROUP, pl.ds(h % GROUP, 1), :] = vol_line[
             h * LANE : (h + 1) * LANE
@@ -276,61 +339,110 @@
         for a in range(COMP):
             out_ref[a, q] = local[a] + (tm_ref[t, t] * own[a, q]) * vol[q]
 
-    def boundary(start):
+    answered = jnp.where(t == 0, last, jnp.where(t < last, 1, 0))
+    answered = answered + jnp.where(r < n_row - 1, 1, 0)
+
+    @pl.when(answered > 0)
+    def _():
+        pl.semaphore_wait(ready.at[0], answered)
+
+    for o in range(1, n_inst):
+
+        @pl.when(jnp.logical_not(inst_first(o)))
+        def _(o=o):
+            inst_copy(o).start()
+
+    @pl.when(r < n_row - 1)
+    def _():
+        start(to_above())
+
+    @pl.when(jnp.logical_not(up_first))
+    def _():
+        pl.semaphore_wait(ready.at[1], 1)
+        start(to_up())
+
+    @pl.when(jnp.logical_not(down_first))
+    def _():
+        pl.semaphore_wait(ready.at[2], 1)
+        start(to_down())
+
+    def arrived(slot):
+        pltpu.make_async_copy(ghost.at[slot], ghost.at[slot], ghost_recv.at[slot]).wait()
+
+    def boundary(slot):
+        cell = side(slot, lambda k: ghost_cell[slot, :, k ^ 1, :])
+        values = gathered(ghost.at[slot], cell)
+        if slot == LATE:
+            block = lambda i: late_jac[i - COMP * COMP]
+        else:
+            block = lambda i: side(slot, lambda k: bound[i, :, k, :])
+        flux = applied(block, COMP * COMP, values)
+        for a in range(COMP):
+            inner = side(slot, lambda k, a=a: inner_flux[a, :, k, :])
+            first, rest = two_terms(inner + flux[a])
+            bound_terms[slot, a] = first
+            bound_terms[slot, COMP + a] = rest
         for j in range(b_tiles):
-            at = slice(j * LANE, (j + 1) * LANE)
-            outer = [
-                ghost_in[j, pl.ds(8 * start + b, 2, stride=8), :] for b in range(COMP)
-            ]
-            block = lambda i, at=at: bound[i, start : start + 2, at]
-            flux = applied(block, COMP * COMP, outer)
-            for a in range(COMP):
-                first, rest = two_terms(inner_flux[j][a][start : start + 2] + flux[a])
-                bound_terms[a, j, start : start + 2, :] = first
-                bound_terms[COMP + a, j, start : start + 2, :] = rest
-            for k in range(start, start + 2):
-                place = boundary_place(j, k)
-                mask = chunk_mask(bcell[k : k + 1, at])
-                for a in range(TERMS):
-                    value = packed_row(bound_terms[a, j, pl.ds(k, 1), :])
-                    rows[a * PACK : (a + 1) * PACK, place : place + LANE] = jnp.where(
-                        mask, value, jnp.bfloat16(0)
-                    )
+            place = boundary_place(slot, j)
+            mask = chunk_mask(place_cell[slot, j : j + 1, :])
+            for a in range(TERMS):
+                value = packed_row(bound_terms[slot, a, j : j + 1, :])
+                rows[a * PACK : (a + 1) * PACK, place : place + LANE] = jnp.where(
+                    mask, value, jnp.bfloat16(0)
+                )
 
     @pl.when(r > 0)
     def _():
-        ghost_copy(2, row=r - 1).wait_send()
-        half = ghost_in.at[:, 16 : 16 + COMP]
-        pltpu.make_async_copy(half, half, ghost_recv.at[2]).wait()
+        arrived(BELOW)
 
     @pl.when(r < n_row - 1)
     def _():
-        ghost_copy(3, row=r + 1).wait_send()
-        half = ghost_in.at[:, 24 : 24 + COMP]
-        pltpu.make_async_copy(half, half, ghost_recv.at[3]).wait()
-
-    boundary(2)
+        arrived(ABOVE)
+
+    boundary(ABOVE)
+    boundary(BELOW)
     acc[...] = acc[...] + product(2 * faces, 2 * bounds)
 
-    for c in sends:
-        c.wait()
+    arrived(NEAR)
+    boundary(NEAR)
+    acc[...] = acc[...] + product(boundary_place(NEAR, 0), bounds)
+
+    if n_inst > 1:
+        others = dirs.at[1:n_inst]
+        pltpu.make_async_copy(others, others, inst_recv.at[0]).wait()
     weights = [tm_ref[t, lax.rem(t + n_inst - o, n_inst)] for o in range(1, n_inst)]
     for q in range(blocks):
         for a in range(COMP):
+            at = a * PACK + q * GROUP
+            both = acc[at : at + GROUP, :]
+            at = at + COMP * PACK
+            both = both + acc[at : at + GROUP, :]
             mixed = None
             for o in range(1, n_inst):
                 term = weights[o - 1] * dirs[o, a, q]
                 mixed = term if mixed is None else mixed + term
-            at = a * PACK + q * GROUP
-            both = acc[at : at + GROUP, :]
-            at = at + COMP * PACK
-            both = both + acc[at : at + GROUP, :]
-            out_ref[a, q] = out_ref[a, q] + mixed * vol[q] + both
-
-    to_down.wait()
-    to_up.wait()
-    boundary(0)
-    acc[...] = product(2 * faces + 2 * bounds, 2 * bounds)
+            if mixed is not None:
+                both = mixed * vol[q] + both
+            out_ref[a, q] = out_ref[a, q] + both
+
+    for o in range(1, n_inst):
+        inst_copy(o).wait_send()
+    for c in to_up() + to_down():
+        c.wait_send()
+
+    @pl.when(r > 0)
+    def _():
+        for c in to_below():
+            c.wait_send()
+
+    @pl.when(r < n_row - 1)
+    def _():
+        for c in to_above():
+            c.wait_send()
+
+    arrived(LATE)
+    boundary(LATE)
+    acc[...] = product(boundary_place(LATE, 0), bounds)
     for q in range(blocks):
         for a in range(COMP):
             at = a * PACK + q * GROUP
@@ -363,7 +475,14 @@
     width = 2 * faces + 4 * bounds
     f32, i32, bf16 = jnp.float32, jnp.int32, jnp.bfloat16
     cell_view = (blocks, GROUP, LANE)
+    bound_view = (b_tiles, 4, LANE)
     hbm = pl.BlockSpec(memory_space=pl.ANY)
+
+    def by_tile(cell):
+        return cell.reshape(4, b_tiles, LANE).transpose(1, 0, 2)
+
+    index_rows = pl.cdiv(b_tiles * 4, blocks * GROUP)
+    assert index_rows * blocks * GROUP == b_tiles * 4
     result = pl.pallas_call(
         functools.partial(kernel, n_inst, n_row, n_pitch),
         out_shape=pltpu.VMEM((COMP, *cell_view), f32),
@@ -378,22 +497,22 @@
             pltpu.VMEM((50, f_tiles, LANE), f32),
             pltpu.VMEM((f_tiles, LANE), i32),
             pltpu.VMEM((f_tiles, LANE), i32),
-            pltpu.VMEM((50, 4, bounds), f32),
-            pltpu.VMEM((4, bounds), i32),
-            pltpu.VMEM((4, bounds), i32),
+            pltpu.VMEM((50, *bound_view), f32),
+            pltpu.VMEM(bound_view, i32),
             pltpu.VMEM((n_inst, COMP, *cell_view), f32),
-            pltpu.VMEM((b_tiles, 32, LANE), f32),
-            pltpu.VMEM((b_tiles, 32, LANE), f32),
+            pltpu.VMEM((4, COMP + index_rows, *cell_view), f32),
+            pltpu.VMEM((4, *bound_view), i32),
+            pltpu.VMEM((25, b_tiles, LANE), f32),
+            pltpu.VMEM((COMP, *bound_view), f32),
+            pltpu.VMEM((4, b_tiles, LANE), i32),
             pltpu.VMEM((TERMS, f_tiles, LANE), f32),
-            pltpu.VMEM((TERMS, b_tiles, GROUP, LANE), f32),
+            pltpu.VMEM((4, TERMS, b_tiles, LANE), f32),
             pltpu.VMEM((TERMS * PACK, width), bf16),
             pltpu.VMEM((LANE, width), bf16),
             pltpu.VMEM((TERMS * PACK, LANE), f32),
-            pltpu.SemaphoreType.DMA((10,)),
-            pltpu.SemaphoreType.DMA((n_inst,)),
-            pltpu.SemaphoreType.DMA((n_inst,)),
+            pltpu.SemaphoreType.DMA((1,)),
             pltpu.SemaphoreType.DMA((4,)),
-            pltpu.SemaphoreType.DMA((4,)),
+            pltpu.SemaphoreType.REGULAR((3,)),
         ],
         compiler_params=pltpu.CompilerParams(collective_id=0, has_side_effects=True),
     )(
@@ -404,9 +523,9 @@
         face_jac[0].reshape(50, f_tiles, LANE),
         face_left.reshape(f_tiles, LANE),
         face_right.reshape(f_tiles, LANE),
-        bound_jac[0].transpose(1, 0, 2),
-        bound_cell,
-        send_cell,
+        bound_jac[0].reshape(4, 50, b_tiles, LANE).transpose(1, 2, 0, 3),
+        by_tile(bound_cell),
+        by_tile(send_cell),
     )
     return result.reshape(1, COMP, cells)
 

time: 10.7 us -> 9.19 us (0.86)
  the two profiles are of different devices: /device:TPU:0 before, /device:TPU:18 now
where the time goes in v1:
time: 9.19 us; the launch traced here: 9.05 us
  Pallas kernels  8.43 us (92%)
  local copies, waits for them, and re-layouts  0.61 us (7%)
    pallas_call x1, Pallas kernels, per_device(): pl.pallas_call(functools.partial(kernel, n_inst, n_row, n_pitch), out_sha...  8.43 us
    unnamed x1, local copies, waits for them, and re-layouts  0.61 us

profile of v1, /device:TPU:18, one launch (start us, length us, event | category | flops | bytes accessed | tf_op | source)
XLA Modules:
  0.0 9.0 jit_solution(5177116880252320508)
XLA Ops:
  0.0 8.4 %shard_map.100 = f32[5,3,4,128]{3,2,1,0:T(4,128)S(1)} custom-call(f32[4,4]{1,0:T(4,128)} %refs_0_.1, f32[5,3,4,128]{3,2,1,0:T(4,128)} %bitcast.19, f32[1536]{0:T(1024)} %refs_2_.1, f32[25,3,4,128]{3,2,1,0:T(4,128)} %bitcast.18, f32[50,24,128]{2,1,0:T(8,128)} %bitcast.16, s32[24,128]{1,0:T(8,128)} %bitcast.20, s32[24,128]{1,0:T(8,128)} %bitcast.21, ...), custom_call_target="tpu_custom_call" | custom-call | tf_op jit(solution)/shard_map/pallas_call | solution.py:486
  8.4 0.6 %copy.14 = f32[1,5,1536]{2,0,1:T(1,128)} copy(f32[1,5,1536]{2,0,1:T(1,128)S(1)} %bitcast.15) | data formatting | bytes 61440

commit v2 on v1

--- a/solution.py
+++ b/solution.py
@@ -104,6 +104,7 @@
     right,
     bound,
     bcell,
+    scell,
     dirs,
     ghost,
     ghost_cell,
@@ -140,8 +141,10 @@
     up = lax.rem(p + 1, n_pitch)
     down = lax.rem(p + n_pitch - 1, n_pitch)
 
-    down_first = jnp.logical_and(p >= 1, p <= n_pitch - 2)
-    up_first = p >= n_pitch - 2
+    down_first = jnp.logical_and(p >= 1, jnp.logical_or(p < n_pitch - 1, t > 0))
+    up_first = jnp.logical_or(
+        p == n_pitch - 1, jnp.logical_and(p == n_pitch - 2, t == 0)
+    )
 
     @pl.when(jnp.logical_not(down_first))
     def _():
@@ -167,6 +170,7 @@
     pairs = [
         (dir_hbm, own),
         (bcell_hbm, bcell),
+        (scell_hbm, scell),
         (left_hbm, left),
         (right_hbm, right),
         (face_hbm, face),
@@ -179,7 +183,7 @@
         pltpu.make_async_copy(a, b, local_sem.at[i]) for i, (a, b) in enumerate(pairs)
     ]
 
-    def ghost_copies(slot, at, **place):
+    def ghost_copies(slot, at, early, **place):
         return [
             pltpu.make_async_remote_copy(
                 src_ref=a,
@@ -190,29 +194,34 @@
                 device_id_type=MESH,
             )
             for i, (a, b) in enumerate(
-                [(dir_hbm, ghost.at[slot, 0:COMP]), (scell_hbm, ghost_cell.at[slot])]
+                [
+                    (dir_hbm if early else own, ghost.at[slot, 0:COMP]),
+                    (scell_hbm if early else scell, ghost_cell.at[slot]),
+                ]
             )
         ]
 
-    def to_up():
-        return ghost_copies(jnp.where(p == n_pitch - 1, LATE, NEAR), n_inst, pitch=up)
-
-    def to_down():
-        return ghost_copies(jnp.where(p == 1, NEAR, LATE), n_inst + 2, pitch=down)
+    def to_up(early=False):
+        slot = jnp.where(p == n_pitch - 1, LATE, NEAR)
+        return ghost_copies(slot, n_inst, early, pitch=up)
+
+    def to_down(early=False):
+        slot = jnp.where(p == 1, NEAR, LATE)
+        return ghost_copies(slot, n_inst + 2, early, pitch=down)
 
     def to_below():
-        return ghost_copies(ABOVE, n_inst + 4, row=r - 1)
+        return ghost_copies(ABOVE, n_inst + 4, True, row=r - 1)
 
     def to_above():
-        return ghost_copies(BELOW, n_inst + 6, row=r + 1)
+        return ghost_copies(BELOW, n_inst + 6, False, row=r + 1)
 
     def start(group):
         for c in group:
             c.start()
 
-    def inst_copy(o):
+    def inst_copy(o, early=False):
         return pltpu.make_async_remote_copy(
-            src_ref=dir_hbm,
+            src_ref=dir_hbm if early else own,
             dst_ref=dirs.at[o],
             send_sem=send_sem.at[o],
             recv_sem=inst_recv.at[0],
@@ -233,19 +242,19 @@
 
     @pl.when(up_first)
     def _():
-        start(to_up())
+        start(to_up(True))
         signal(ready.at[2], pitch=up)
 
     for o in range(1, n_inst):
 
         @pl.when(inst_first(o))
         def _(o=o):
-            inst_copy(o).start()
-            signal(ready.at[0], inst=lax.rem(t + o, n_inst))
+            inst_copy(o, True).start()
+            signal(ready.at[jnp.where(t == last, 3, 0)], inst=lax.rem(t + o, n_inst))
 
     @pl.when(down_first)
     def _():
-        start(to_down())
+        start(to_down(True))
         signal(ready.at[1], pitch=down)
 
     @pl.when(r > 0)
@@ -339,17 +348,16 @@
         for a in range(COMP):
             out_ref[a, q] = local[a] + (tm_ref[t, t] * own[a, q]) * vol[q]
 
-    answered = jnp.where(t == 0, last, jnp.where(t < last, 1, 0))
+    answered = jnp.where(t == 0, max(n_inst - 2, 0), 0)
     answered = answered + jnp.where(r < n_row - 1, 1, 0)
 
     @pl.when(answered > 0)
     def _():
         pl.semaphore_wait(ready.at[0], answered)
 
-    for o in range(1, n_inst):
-
-        @pl.when(jnp.logical_not(inst_first(o)))
-        def _(o=o):
+    @pl.when(t == 0)
+    def _():
+        for o in range(1, last):
             inst_copy(o).start()
 
     @pl.when(r < n_row - 1)
@@ -361,10 +369,27 @@
         pl.semaphore_wait(ready.at[1], 1)
         start(to_up())
 
-    @pl.when(jnp.logical_not(down_first))
-    def _():
+    def answer_down():
         pl.semaphore_wait(ready.at[2], 1)
         start(to_down())
+
+    @pl.when(jnp.logical_and(p > 0, jnp.logical_not(down_first)))
+    def _():
+        answer_down()
+
+    @pl.when(t < last)
+    def _():
+        pl.semaphore_wait(ready.at[3], 1)
+        for o in range(1, n_inst):
+            u = lax.rem(t + o, n_inst)
+
+            @pl.when(jnp.logical_or(u == last, jnp.logical_and(t > 0, u > 0)))
+            def _(o=o):
+                inst_copy(o).start()
+
+    @pl.when(p == 0)
+    def _():
+        answer_down()
 
     def arrived(slot):
         pltpu.make_async_copy(ghost.at[slot], ghost.at[slot], ghost_recv.at[slot]).wait()
@@ -407,6 +432,12 @@
     boundary(NEAR)
     acc[...] = acc[...] + product(boundary_place(NEAR, 0), bounds)
 
+    @pl.when(p > 0)
+    def _():
+        arrived(LATE)
+        boundary(LATE)
+        acc[...] = acc[...] + product(boundary_place(LATE, 0), bounds)
+
     if n_inst > 1:
         others = dirs.at[1:n_inst]
         pltpu.make_async_copy(others, others, inst_recv.at[0]).wait()
@@ -425,6 +456,18 @@
                 both = mixed * vol[q] + both
             out_ref[a, q] = out_ref[a, q] + both
 
+    @pl.when(p == 0)
+    def _():
+        arrived(LATE)
+        boundary(LATE)
+        acc[...] = product(boundary_place(LATE, 0), bounds)
+        for q in range(blocks):
+            for a in range(COMP):
+                at = a * PACK + q * GROUP
+                both = acc[at : at + GROUP, :]
+                at = at + COMP * PACK
+                out_ref[a, q] = out_ref[a, q] + (both + acc[at : at + GROUP, :])
+
     for o in range(1, n_inst):
         inst_copy(o).wait_send()
     for c in to_up() + to_down():
@@ -439,16 +482,6 @@
     def _():
         for c in to_above():
             c.wait_send()
-
-    arrived(LATE)
-    boundary(LATE)
-    acc[...] = product(boundary_place(LATE, 0), bounds)
-    for q in range(blocks):
-        for a in range(COMP):
-            at = a * PACK + q * GROUP
-            both = acc[at : at + GROUP, :]
-            at = at + COMP * PACK
-            out_ref[a, q] = out_ref[a, q] + (both + acc[at : at + GROUP, :])
 
 
 def per_device(
@@ -499,6 +532,7 @@
             pltpu.VMEM((f_tiles, LANE), i32),
             pltpu.VMEM((50, *bound_view), f32),
             pltpu.VMEM(bound_view, i32),
+            pltpu.VMEM(bound_view, i32),
             pltpu.VMEM((n_inst, COMP, *cell_view), f32),
             pltpu.VMEM((4, COMP + index_rows, *cell_view), f32),
             pltpu.VMEM((4, *bound_view), i32),
@@ -512,7 +546,7 @@
             pltpu.VMEM((TERMS * PACK, LANE), f32),
             pltpu.SemaphoreType.DMA((1,)),
             pltpu.SemaphoreType.DMA((4,)),
-            pltpu.SemaphoreType.REGULAR((3,)),
+            pltpu.SemaphoreType.REGULAR((4,)),
         ],
         compiler_params=pltpu.CompilerParams(collective_id=0, has_side_effects=True),
     )(

time: 9.19 us -> 8.68 us (0.945)
  the two profiles are of different devices: /device:TPU:18 before, /device:TPU:0 now
where the time goes in v2:
time: 8.68 us; the launch traced here: 8.53 us
  Pallas kernels  7.91 us (91%)
  local copies, waits for them, and re-layouts  0.61 us (7%)
    pallas_call x1, Pallas kernels, per_device(): pl.pallas_call(functools.partial(kernel, n_inst, n_row, n_pitch), out_sha...  7.91 us
    unnamed x1, local copies, waits for them, and re-layouts  0.61 us

profile of v2, /device:TPU:0, one launch (start us, length us, event | category | flops | bytes accessed | tf_op | source)
XLA Modules:
  0.0 8.5 jit_solution(11990635745078790054)
XLA Ops:
  0.0 7.9 %shard_map.100 = f32[5,3,4,128]{3,2,1,0:T(4,128)S(1)} custom-call(f32[4,4]{1,0:T(4,128)} %refs_0_.1, f32[5,3,4,128]{3,2,1,0:T(4,128)} %bitcast.19, f32[1536]{0:T(1024)} %refs_2_.1, f32[25,3,4,128]{3,2,1,0:T(4,128)} %bitcast.18, f32[50,24,128]{2,1,0:T(8,128)} %bitcast.16, s32[24,128]{1,0:T(8,128)} %bitcast.20, s32[24,128]{1,0:T(8,128)} %bitcast.21, ...), custom_call_target="tpu_custom_call" | custom-call | tf_op jit(solution)/shard_map/pallas_call | solution.py:519
  7.9 0.6 %copy.14 = f32[1,5,1536]{2,0,1:T(1,128)} copy(f32[1,5,1536]{2,0,1:T(1,128)S(1)} %bitcast.15) | data formatting | bytes 61440

commit v3 on v2

--- a/solution.py
+++ b/solution.py
@@ -69,6 +69,7 @@
 
 
 NEAR, LATE, BELOW, ABOVE = 0, 1, 2, 3
+ORDER = (2, 3, 1, 0)
 
 
 def kernel(n_inst, n_row, n_pitch, *refs):
@@ -205,9 +206,9 @@
         slot = jnp.where(p == n_pitch - 1, LATE, NEAR)
         return ghost_copies(slot, n_inst, early, pitch=up)
 
-    def to_down(early=False):
+    def to_down():
         slot = jnp.where(p == 1, NEAR, LATE)
-        return ghost_copies(slot, n_inst + 2, early, pitch=down)
+        return ghost_copies(slot, n_inst + 2, False, pitch=down)
 
     def to_below():
         return ghost_copies(ABOVE, n_inst + 4, True, row=r - 1)
@@ -240,22 +241,26 @@
     def _():
         pl.semaphore_wait(barrier, greeted)
 
+    leads = jnp.logical_and(p == n_pitch - 1, r == 0)
+
     @pl.when(up_first)
     def _():
+        signal(ready.at[1], pitch=up)
+
+    @pl.when(leads)
+    def _():
         start(to_up(True))
-        signal(ready.at[2], pitch=up)
 
     for o in range(1, n_inst):
 
         @pl.when(inst_first(o))
         def _(o=o):
             inst_copy(o, True).start()
-            signal(ready.at[jnp.where(t == last, 3, 0)], inst=lax.rem(t + o, n_inst))
+            signal(ready.at[jnp.where(t == last, 2, 0)], inst=lax.rem(t + o, n_inst))
 
     @pl.when(down_first)
     def _():
-        start(to_down(True))
-        signal(ready.at[1], pitch=down)
+        signal(ready.at[0], pitch=down)
 
     @pl.when(r > 0)
     def _():
@@ -274,7 +279,18 @@
         ghost[ABOVE] = jnp.zeros(ghost.shape[1:], jnp.float32)
         ghost_cell[ABOVE] = jnp.zeros(ghost_cell.shape[1:], jnp.int32)
 
-    for c in copies:
+    for c in copies[0:3]:
+        c.wait()
+
+    @pl.when(jnp.logical_and(up_first, jnp.logical_not(leads)))
+    def _():
+        start(to_up())
+
+    @pl.when(down_first)
+    def _():
+        start(to_down())
+
+    for c in copies[3:]:
         c.wait()
 
     def product(start, size):
@@ -324,7 +340,7 @@
         return jnp.where(edge, pick(0), pick(1))
 
     def boundary_place(slot, j):
-        return 2 * faces + ((3 - slot) * b_tiles + j) * LANE
+        return 2 * faces + (ORDER[slot] * b_tiles + j) * LANE
 
     for j in range(b_tiles):
         block = lambda i, j=j: bound[i, j]
@@ -334,7 +350,10 @@
     for slot in range(4):
         place_cell[slot] = side(slot, lambda k: bcell[:, k, :])
         for j in range(b_tiles):
-            hot_tile(hot, boundary_place(slot, j), place_cell[slot, j : j + 1, :], 1.0)
+            place = boundary_place(slot, j)
+            hot_tile(hot, place, place_cell[slot, j : j + 1, :], 1.0)
+            if slot == LATE:
+                hot[:, place + bounds : place + bounds + LANE] = hot[:, place : place + LANE]
     for i in range(COMP * COMP):
         late_jac[i] = side(LATE, lambda k, i=i: bound[COMP * COMP + i, :, k, :])
 
@@ -350,6 +369,7 @@
 
     answered = jnp.where(t == 0, max(n_inst - 2, 0), 0)
     answered = answered + jnp.where(r < n_row - 1, 1, 0)
+    answered = answered + jnp.where(up_first, 0, 1)
 
     @pl.when(answered > 0)
     def _():
@@ -366,20 +386,19 @@
 
     @pl.when(jnp.logical_not(up_first))
     def _():
+        start(to_up())
+
+    def answer_down():
         pl.semaphore_wait(ready.at[1], 1)
-        start(to_up())
-
-    def answer_down():
+        start(to_down())
+
+    @pl.when(jnp.logical_and(p > 0, jnp.logical_not(down_first)))
+    def _():
+        answer_down()
+
+    @pl.when(t < last)
+    def _():
         pl.semaphore_wait(ready.at[2], 1)
-        start(to_down())
-
-    @pl.when(jnp.logical_and(p > 0, jnp.logical_not(down_first)))
-    def _():
-        answer_down()
-
-    @pl.when(t < last)
-    def _():
-        pl.semaphore_wait(ready.at[3], 1)
         for o in range(1, n_inst):
             u = lax.rem(t + o, n_inst)
 
@@ -396,25 +415,38 @@
 
     def boundary(slot):
         cell = side(slot, lambda k: ghost_cell[slot, :, k ^ 1, :])
-        values = gathered(ghost.at[slot], cell)
-        if slot == LATE:
-            block = lambda i: late_jac[i - COMP * COMP]
-        else:
-            block = lambda i: side(slot, lambda k: bound[i, :, k, :])
-        flux = applied(block, COMP * COMP, values)
+        total = [side(slot, lambda k, a=a: inner_flux[a, :, k, :]) for a in range(COMP)]
+        for b, value in enumerate(gathered(ghost.at[slot], cell)):
+            for a in range(COMP):
+                i = COMP * a + b
+                if slot == LATE:
+                    block = late_jac[i]
+                else:
+                    block = side(slot, lambda k: bound[COMP * COMP + i, :, k, :])
+                total[a] = total[a] + block * value
         for a in range(COMP):
-            inner = side(slot, lambda k, a=a: inner_flux[a, :, k, :])
-            first, rest = two_terms(inner + flux[a])
+            first, rest = two_terms(total[a])
             bound_terms[slot, a] = first
             bound_terms[slot, COMP + a] = rest
         for j in range(b_tiles):
-            place = boundary_place(slot, j)
             mask = chunk_mask(place_cell[slot, j : j + 1, :])
             for a in range(TERMS):
                 value = packed_row(bound_terms[slot, a, j : j + 1, :])
-                rows[a * PACK : (a + 1) * PACK, place : place + LANE] = jnp.where(
+                term, place = a, boundary_place(slot, j)
+                if slot == LATE and a >= COMP:
+                    term, place = a - COMP, place + bounds
+                rows[term * PACK : (term + 1) * PACK, place : place + LANE] = jnp.where(
                     mask, value, jnp.bfloat16(0)
                 )
+
+    def late_product():
+        at = slice(boundary_place(LATE, 0), boundary_place(LATE, 0) + 2 * bounds)
+        return lax.dot_general(
+            rows[0 : COMP * PACK, at],
+            hot[:, at],
+            (((1,), (1,)), ((), ())),
+            preferred_element_type=jnp.float32,
+        )
 
     @pl.when(r > 0)
     def _():
@@ -436,7 +468,7 @@
     def _():
         arrived(LATE)
         boundary(LATE)
-        acc[...] = acc[...] + product(boundary_place(LATE, 0), bounds)
+        acc[0 : COMP * PACK] = acc[0 : COMP * PACK] + late_product()
 
     if n_inst > 1:
         others = dirs.at[1:n_inst]
@@ -460,13 +492,11 @@
     def _():
         arrived(LATE)
         boundary(LATE)
-        acc[...] = product(boundary_place(LATE, 0), bounds)
+        acc[0 : COMP * PACK] = late_product()
         for q in range(blocks):
             for a in range(COMP):
                 at = a * PACK + q * GROUP
-                both = acc[at : at + GROUP, :]
-                at = at + COMP * PACK
-                out_ref[a, q] = out_ref[a, q] + (both + acc[at : at + GROUP, :])
+                out_ref[a, q] = out_ref[a, q] + acc[at : at + GROUP, :]
 
     for o in range(1, n_inst):
         inst_copy(o).wait_send()
@@ -505,7 +535,7 @@
     blocks = cells // (GROUP * LANE)
     f_tiles = faces // LANE
     b_tiles = bounds // LANE
-    width = 2 * faces + 4 * bounds
+    width = 2 * faces + 5 * bounds
     f32, i32, bf16 = jnp.float32, jnp.int32, jnp.bfloat16
     cell_view = (blocks, GROUP, LANE)
     bound_view = (b_tiles, 4, LANE)
@@ -546,7 +576,7 @@
             pltpu.VMEM((TERMS * PACK, LANE), f32),
             pltpu.SemaphoreType.DMA((1,)),
             pltpu.SemaphoreType.DMA((4,)),
-            pltpu.SemaphoreType.REGULAR((4,)),
+            pltpu.SemaphoreType.REGULAR((3,)),
         ],
         compiler_params=pltpu.CompilerParams(collective_id=0, has_side_effects=True),
     )(

time: 8.68 us -> 8.55 us (0.985)
  Pallas kernels: 7.91 us -> 7.79 us
    pallas_call x1, Pallas kernels: 7.91 us -> 7.79 us  [per_device(): pl.pallas_call(functools.partial(kernel, n_inst, n_row, n_pitch), out_sha...]
where the time goes in v3:
time: 8.55 us; the launch traced here: 8.41 us
  Pallas kernels  7.79 us (91%)
  local copies, waits for them, and re-layouts  0.61 us (7%)
    pallas_call x1, Pallas kernels, per_device(): pl.pallas_call(functools.partial(kernel, n_inst, n_row, n_pitch), out_sha...  7.79 us
    unnamed x1, local copies, waits for them, and re-layouts  0.61 us

profile of v3, /device:TPU:0, one launch (start us, length us, event | category | flops | bytes accessed | tf_op | source)
XLA Modules:
  0.0 8.4 jit_solution(5888712803321484438)
XLA Ops:
  0.0 7.8 %shard_map.100 = f32[5,3,4,128]{3,2,1,0:T(4,128)S(1)} custom-call(f32[4,4]{1,0:T(4,128)} %refs_0_.1, f32[5,3,4,128]{3,2,1,0:T(4,128)} %bitcast.19, f32[1536]{0:T(1024)} %refs_2_.1, f32[25,3,4,128]{3,2,1,0:T(4,128)} %bitcast.18, f32[50,24,128]{2,1,0:T(8,128)} %bitcast.16, s32[24,128]{1,0:T(8,128)} %bitcast.20, s32[24,128]{1,0:T(8,128)} %bitcast.21, ...), custom_call_target="tpu_custom_call" | custom-call | tf_op jit(solution)/shard_map/pallas_call | solution.py:549
  7.8 0.6 %copy.14 = f32[1,5,1536]{2,0,1:T(1,128)} copy(f32[1,5,1536]{2,0,1:T(1,128)S(1)} %bitcast.15) | data formatting | bytes 61440

commit v4 on v3

--- a/solution.py
+++ b/solution.py
@@ -110,6 +110,7 @@
     ghost,
     ghost_cell,
     late_jac,
+    late_hot,
     inner_flux,
     place_cell,
     flux_terms,
@@ -155,19 +156,6 @@
     def _():
         signal(barrier, pitch=up)
 
-    @pl.when(r < n_row - 1)
-    def _():
-        signal(barrier, row=r + 1)
-
-    @pl.when(t == 0)
-    def _():
-        for u in range(1, n_inst):
-            signal(barrier, inst=u)
-
-    @pl.when(jnp.logical_and(t > 0, t < last))
-    def _():
-        signal(barrier, inst=last)
-
     pairs = [
         (dir_hbm, own),
         (bcell_hbm, bcell),
@@ -233,21 +221,40 @@
     def inst_first(o):
         return jnp.logical_or(lax.rem(t + o, n_inst) == 0, t == last)
 
+    leads = jnp.logical_and(p == n_pitch - 1, r == 0)
+    first = jnp.logical_and(leads, t == 0)
+
+    @pl.when(first)
+    def _():
+        pl.semaphore_wait(barrier, 1)
+        start(to_up(True))
+
+    @pl.when(r < n_row - 1)
+    def _():
+        signal(barrier, row=r + 1)
+
+    @pl.when(t == 0)
+    def _():
+        for u in range(1, n_inst):
+            signal(barrier, inst=u)
+
+    @pl.when(jnp.logical_and(t > 0, t < last))
+    def _():
+        signal(barrier, inst=last)
+
     greeted = jnp.where(t == last, last, jnp.where(t > 0, 1, 0))
     greeted = greeted + jnp.where(r > 0, 1, 0)
     greeted = greeted + jnp.where(down_first, 1, 0) + jnp.where(up_first, 1, 0)
 
-    @pl.when(greeted > 0)
+    @pl.when(jnp.logical_and(greeted > 0, jnp.logical_not(first)))
     def _():
         pl.semaphore_wait(barrier, greeted)
 
-    leads = jnp.logical_and(p == n_pitch - 1, r == 0)
-
     @pl.when(up_first)
     def _():
         signal(ready.at[1], pitch=up)
 
-    @pl.when(leads)
+    @pl.when(jnp.logical_and(leads, jnp.logical_not(first)))
     def _():
         start(to_up(True))
 
@@ -353,7 +360,10 @@
             place = boundary_place(slot, j)
             hot_tile(hot, place, place_cell[slot, j : j + 1, :], 1.0)
             if slot == LATE:
-                hot[:, place + bounds : place + bounds + LANE] = hot[:, place : place + LANE]
+                turned = hot[:, place : place + LANE].astype(jnp.float32).T
+                turned = turned.astype(jnp.bfloat16)
+                late_hot[j * LANE : (j + 1) * LANE, :] = turned
+                late_hot[bounds + j * LANE : bounds + (j + 1) * LANE, :] = turned
     for i in range(COMP * COMP):
         late_jac[i] = side(LATE, lambda k, i=i: bound[COMP * COMP + i, :, k, :])
 
@@ -443,8 +453,8 @@
         at = slice(boundary_place(LATE, 0), boundary_place(LATE, 0) + 2 * bounds)
         return lax.dot_general(
             rows[0 : COMP * PACK, at],
-            hot[:, at],
-            (((1,), (1,)), ((), ())),
+            late_hot[...],
+            (((1,), (0,)), ((), ())),
             preferred_element_type=jnp.float32,
         )
 
@@ -567,6 +577,7 @@
             pltpu.VMEM((4, COMP + index_rows, *cell_view), f32),
             pltpu.VMEM((4, *bound_view), i32),
             pltpu.VMEM((25, b_tiles, LANE), f32),
+            pltpu.VMEM((2 * bounds, LANE), bf16),
             pltpu.VMEM((COMP, *bound_view), f32),
             pltpu.VMEM((4, b_tiles, LANE), i32),
             pltpu.VMEM((TERMS, f_tiles, LANE), f32),

time: 8.55 us -> 8.53 us (level)
  no operation moved by 1% of the time
where the time goes in v4:
time: 8.53 us; the launch traced here: 8.39 us
  Pallas kernels  7.77 us (91%)
  local copies, waits for them, and re-layouts  0.61 us (7%)
    pallas_call x1, Pallas kernels, per_device(): pl.pallas_call(functools.partial(kernel, n_inst, n_row, n_pitch), out_sha...  7.77 us
    unnamed x1, local copies, waits for them, and re-layouts  0.61 us

profile of v4, /device:TPU:0, one launch (start us, length us, event | category | flops | bytes accessed | tf_op | source)
XLA Modules:
  0.0 8.4 jit_solution(14281291065022627513)
XLA Ops:
  0.0 7.8 %shard_map.100 = f32[5,3,4,128]{3,2,1,0:T(4,128)S(1)} custom-call(f32[4,4]{1,0:T(4,128)} %refs_0_.1, f32[5,3,4,128]{3,2,1,0:T(4,128)} %bitcast.19, f32[1536]{0:T(1024)} %refs_2_.1, f32[25,3,4,128]{3,2,1,0:T(4,128)} %bitcast.18, f32[50,24,128]{2,1,0:T(8,128)} %bitcast.16, s32[24,128]{1,0:T(8,128)} %bitcast.20, s32[24,128]{1,0:T(8,128)} %bitcast.21, ...), custom_call_target="tpu_custom_call" | custom-call | tf_op jit(solution)/shard_map/pallas_call | solution.py:559
  7.8 0.6 %copy.14 = f32[1,5,1536]{2,0,1:T(1,128)} copy(f32[1,5,1536]{2,0,1:T(1,128)S(1)} %bitcast.15) | data formatting | bytes 61440

commit v5 on v4

--- a/solution.py
+++ b/solution.py
@@ -111,6 +111,8 @@
     ghost_cell,
     late_jac,
     late_hot,
+    late_value,
+    picked,
     inner_flux,
     place_cell,
     flux_terms,
@@ -223,6 +225,18 @@
 
     leads = jnp.logical_and(p == n_pitch - 1, r == 0)
     first = jnp.logical_and(leads, t == 0)
+    picks = jnp.logical_and(p == n_pitch - 1, r > 0)
+
+    def picked_copy():
+        return pltpu.make_async_remote_copy(
+            src_ref=picked,
+            dst_ref=late_value,
+            send_sem=send_sem.at[n_inst],
+            recv_sem=ghost_recv.at[LATE],
+            device_id={"pitch": up},
+            device_id_type=MESH,
+        )
+
 
     @pl.when(first)
     def _():
@@ -289,9 +303,14 @@
     for c in copies[0:3]:
         c.wait()
 
-    @pl.when(jnp.logical_and(up_first, jnp.logical_not(leads)))
+    @pl.when(jnp.logical_and(up_first, p < n_pitch - 1))
     def _():
         start(to_up())
+
+    @pl.when(picks)
+    def _():
+        for b, value in enumerate(gathered(own, scell[:, 1, :])):
+            picked[b] = value
 
     @pl.when(down_first)
     def _():
@@ -299,6 +318,10 @@
 
     for c in copies[3:]:
         c.wait()
+
+    @pl.when(picks)
+    def _():
+        picked_copy().start()
 
     def product(start, size):
         return lax.dot_general(
@@ -423,10 +446,13 @@
     def arrived(slot):
         pltpu.make_async_copy(ghost.at[slot], ghost.at[slot], ghost_recv.at[slot]).wait()
 
-    def boundary(slot):
+    def ghost_values(slot):
         cell = side(slot, lambda k: ghost_cell[slot, :, k ^ 1, :])
+        return gathered(ghost.at[slot], cell)
+
+    def boundary(slot, values):
         total = [side(slot, lambda k, a=a: inner_flux[a, :, k, :]) for a in range(COMP)]
-        for b, value in enumerate(gathered(ghost.at[slot], cell)):
+        for b, value in enumerate(values):
             for a in range(COMP):
                 i = COMP * a + b
                 if slot == LATE:
@@ -466,18 +492,18 @@
     def _():
         arrived(ABOVE)
 
-    boundary(ABOVE)
-    boundary(BELOW)
+    boundary(ABOVE, ghost_values(ABOVE))
+    boundary(BELOW, ghost_values(BELOW))
     acc[...] = acc[...] + product(2 * faces, 2 * bounds)
 
     arrived(NEAR)
-    boundary(NEAR)
+    boundary(NEAR, ghost_values(NEAR))
     acc[...] = acc[...] + product(boundary_place(NEAR, 0), bounds)
 
     @pl.when(p > 0)
     def _():
         arrived(LATE)
-        boundary(LATE)
+        boundary(LATE, ghost_values(LATE))
         acc[0 : COMP * PACK] = acc[0 : COMP * PACK] + late_product()
 
     if n_inst > 1:
@@ -500,8 +526,17 @@
 
     @pl.when(p == 0)
     def _():
-        arrived(LATE)
-        boundary(LATE)
+        @pl.when(r == 0)
+        def _():
+            arrived(LATE)
+            for b, value in enumerate(ghost_values(LATE)):
+                late_value[b] = value
+
+        @pl.when(r > 0)
+        def _():
+            pltpu.make_async_copy(late_value, late_value, ghost_recv.at[LATE]).wait()
+
+        boundary(LATE, [late_value[b] for b in range(COMP)])
         acc[0 : COMP * PACK] = late_product()
         for q in range(blocks):
             for a in range(COMP):
@@ -510,8 +545,17 @@
 
     for o in range(1, n_inst):
         inst_copy(o).wait_send()
-    for c in to_up() + to_down():
+    for c in to_down():
         c.wait_send()
+
+    @pl.when(jnp.logical_not(picks))
+    def _():
+        for c in to_up():
+            c.wait_send()
+
+    @pl.when(picks)
+    def _():
+        picked_copy().wait_send()
 
     @pl.when(r > 0)
     def _():
@@ -578,6 +622,8 @@
             pltpu.VMEM((4, *bound_view), i32),
             pltpu.VMEM((25, b_tiles, LANE), f32),
             pltpu.VMEM((2 * bounds, LANE), bf16),
+            pltpu.VMEM((COMP, b_tiles, LANE), f32),
+            pltpu.VMEM((COMP, b_tiles, LANE), f32),
             pltpu.VMEM((COMP, *bound_view), f32),
             pltpu.VMEM((4, b_tiles, LANE), i32),
             pltpu.VMEM((TERMS, f_tiles, LANE), f32),

time: 8.53 us -> 8.52 us (level)
  no operation moved by 1% of the time
where the time goes in v5:
time: 8.52 us; the launch traced here: 8.38 us
  Pallas kernels  7.76 us (91%)
  local copies, waits for them, and re-layouts  0.61 us (7%)
    pallas_call x1, Pallas kernels, per_device(): pl.pallas_call(functools.partial(kernel, n_inst, n_row, n_pitch), out_sha...  7.76 us
    unnamed x1, local copies, waits for them, and re-layouts  0.61 us

profile of v5, /device:TPU:0, one launch (start us, length us, event | category | flops | bytes accessed | tf_op | source)
XLA Modules:
  0.0 8.4 jit_solution(14805337049812988017)
XLA Ops:
  0.0 7.8 %shard_map.100 = f32[5,3,4,128]{3,2,1,0:T(4,128)S(1)} custom-call(f32[4,4]{1,0:T(4,128)} %refs_0_.1, f32[5,3,4,128]{3,2,1,0:T(4,128)} %bitcast.19, f32[1536]{0:T(1024)} %refs_2_.1, f32[25,3,4,128]{3,2,1,0:T(4,128)} %bitcast.18, f32[50,24,128]{2,1,0:T(8,128)} %bitcast.16, s32[24,128]{1,0:T(8,128)} %bitcast.20, s32[24,128]{1,0:T(8,128)} %bitcast.21, ...), custom_call_target="tpu_custom_call" | custom-call | tf_op jit(solution)/shard_map/pallas_call | solution.py:603
  7.8 0.6 %copy.14 = f32[1,5,1536]{2,0,1:T(1,128)} copy(f32[1,5,1536]{2,0,1:T(1,128)S(1)} %bitcast.15) | data formatting | bytes 61440
